TPU v7x, 32 devices: a whole 2x2x4 slice. The times are simulated.
32 devices in a mesh: gx: 8 (over z, core), gy: 4 (over y, x).
Axes of the slice: x: 2, y: 2, z: 4, core: 2. Of those that a mesh axis runs over, the one named last changes fastest.
Arguments:
- rhs_field: float32 [128, 64, 128], P('gx', 'gy'), may hold values from -10 to 10
- diag_blocks: bfloat16 [128, 64, 128, 128], P('gx', 'gy'), may hold values from -1 to 4, as said below
- face_lift: bfloat16 [4, 128, 128], replicated, may hold values from -0.5 to 0.5
- face_state: int32 [128, 64, 4], P('gx', 'gy'), may hold values from 0 to 2
- restrict_basis: float32 [128, 8], replicated, may hold values from -0.5 to 0.5
- coarse_inverse: float32 [128, 64, 8, 8], P('gx', 'gy'), may hold values from -0.4 to 1.2
Outputs:
- solution_field: float32 [128, 64, 128], P('gx', 'gy')
- hessenberg: float32 [3, 2], replicated
Inputs may be any that keep to these rules, and one draw needn't show every extreme that they name: `diag_blocks`: each block has diagonal entries between 2 and 4 and small off-diagonal entries.
All inputs are finite; a program needn't handle non-finite values.
Results may differ from a plain program's by a relative error of at most 0.0023.
Values may be sent and summed in bfloat16 or wider, within the bound.
A program may use at most 64 MiB of HBM per device.

v0:
```python
import jax
import jax.numpy as jnp
from jax import lax
from jax.sharding import PartitionSpec as P


def padded_2(block, sides, width):
    for axis, dim in sides:
        count = lax.axis_size(axis)
        forward = [(i, i + 1) for i in range(count - 1)]
        backward = [(target, source) for source, target in forward]
        low = lax.ppermute(
            lax.slice_in_dim(block, block.shape[dim] - width, None, axis=dim), axis, forward
        )
        high = lax.ppermute(lax.slice_in_dim(block, 0, width, axis=dim), axis, backward)
        block = jnp.concatenate([low, block, high], axis=dim)
    return block


def apply_operator(field, diag_blocks, face_lift, face_state):
    rounded = field.astype(jnp.bfloat16)
    local_part = jnp.einsum(
        "ija,ijab->ijb", rounded, diag_blocks, preferred_element_type=jnp.float32
    )
    padded = padded_2(rounded, (("gx", 0), ("gy", 1)), 1)
    neighbours = [padded[:-2, 1:-1], padded[2:, 1:-1], padded[1:-1, :-2], padded[1:-1, 2:]]
    zero_block = jnp.zeros_like(rounded)
    selected = []
    for face in range(4):
        state = face_state[:, :, face][:, :, None]
        other = neighbours[face]
        selected.append(
            jnp.where(state == 1, other, jnp.where(state == 2, other[:, :, ::-1], zero_block))
        )
    stacked = jnp.concatenate(selected, axis=-1)
    width = rounded.shape[2]
    lifted = jnp.dot(
        stacked.reshape(-1, 4 * width),
        face_lift.reshape(4 * width, width),
        preferred_element_type=jnp.float32,
    )
    return local_part + lifted.reshape(field.shape)


def coarse_correct(field, restrict_basis, coarse_inverse):
    high = lax.Precision.HIGHEST
    coarse = jnp.einsum("ija,ak->ijk", field, restrict_basis, precision=high)
    rows_y = coarse.shape[1]
    column = lax.all_gather(coarse, "gy", axis=1, tiled=True)
    centred = column - jnp.mean(column, axis=1, keepdims=True)
    padded = jnp.pad(centred, ((0, 0), (1, 1), (0, 0)))
    smoothed_all = centred + 0.25 * (padded[:, :-2] + padded[:, 2:])
    start = lax.axis_index("gy") * rows_y
    smoothed = lax.dynamic_slice_in_dim(smoothed_all, start, rows_y, 1)
    solved = jnp.einsum("ijk,ijkl->ijl", smoothed, coarse_inverse, precision=high)
    return field + jnp.einsum("ijl,al->ija", solved, restrict_basis, precision=high)


def least_squares(start_len, hess):
    first = jnp.sqrt(hess[0, 0] ** 2 + hess[1, 0] ** 2)
    cos_one = hess[0, 0] / first
    sin_one = hess[1, 0] / first
    upper = cos_one * hess[0, 1] + sin_one * hess[1, 1]
    lower = -sin_one * hess[0, 1] + cos_one * hess[1, 1]
    second = jnp.sqrt(lower**2 + hess[2, 1] ** 2)
    cos_two = lower / second
    coef_two = cos_two * (-sin_one * start_len) / second
    coef_one = (cos_one * start_len - upper * coef_two) / first
    return (coef_one, coef_two)


def body(rhs_field, diag_blocks, face_lift, face_state, restrict_basis, coarse_inverse):
    start_len = jnp.sqrt(lax.psum(jnp.sum(rhs_field * rhs_field), ("gx", "gy")))
    basis = [rhs_field / start_len]
    precon = []
    hess = jnp.zeros((3, 2), jnp.float32)
    for step in range(2):
        precond = coarse_correct(basis[step], restrict_basis, coarse_inverse)
        precon.append(precond)
        image = apply_operator(precond, diag_blocks, face_lift, face_state)
        partial_dots = jnp.stack([jnp.sum(vector * image) for vector in basis])
        coeffs = lax.psum(partial_dots, ("gx", "gy"))
        for index in range(step + 1):
            image = image - coeffs[index] * basis[index]
        length = jnp.sqrt(lax.psum(jnp.sum(image * image), ("gx", "gy")))
        for index in range(step + 1):
            hess = hess.at[index, step].set(coeffs[index])
        hess = hess.at[step + 1, step].set(length)
        if step == 0:
            basis.append(image / length)
    coef_one, coef_two = least_squares(start_len, hess)
    return (coef_one * precon[0] + coef_two * precon[1], hess)


def solution(mesh):
    in_specs = (
        P("gx", "gy", None),
        P("gx", "gy", None, None),
        P(),
        P("gx", "gy", None),
        P(),
        P("gx", "gy", None, None),
    )
    out_specs = (P("gx", "gy", None), P())
    return jax.shard_map(body, mesh=mesh, in_specs=in_specs, out_specs=out_specs, check_vma=False)
```

profile of v0, /device:TPU:0, one launch (start us, length us, event | category | flops | bytes accessed | tf_op | source)
XLA Modules:
  0.0 293.5 jit_solution(4230740229205972593)
XLA Ops:
  0.6 1.6 multiply_reduce_fusion.7
  2.2 42.2 %psum.35 = f32[]{:T(128)} all-reduce(f32[]{:T(128)} %multiply_reduce_fusion.7), channel_id=1, replica_groups=mesh['gx'=8,'gy'=4] {'gx','gy'}, use_global_device_ids=true, to_apply=%region_1.0 | all-reduce | flops 1 | bytes 8 | tf_op jit(solution)/shard_map/psum | solution.py:73
  45.1 0.9 broadcast_divide_fusion.1
  46.0 1.7 fusion.20
  47.7 10.3 %all_gather.6 = f32[16,64,8]{0,2,1:T(8,128)S(1)} all-gather(f32[16,16,8]{0,2,1:T(8,128)S(1)} %fusion.20), channel_id=1, replica_groups=mesh['gx'=8,'gy'=4] {'gy'}, dimensions={1}, use_global_device_ids=true | all-gather | bytes 40960 | tf_op jit(solution)/shard_map/all_gather | solution.py:49
  58.3 1.1 multiply_reduce_fusion.1
  59.4 1.1 fusion.36
  60.5 1.3 collective-permute-start
  61.8 1.3 collective-permute-start.1
  63.1 0.9 fusion.32
  64.1 5.7 %fusion.18 = f32[16,16,1,128]{3,2,1,0:T(1,128)S(1)} fusion(bf16[16,16,128,128]{3,2,1,0:T(8,128)(2,1)} %param.17, bf16[16,16,128,1]{2,1,0,3:T(8,128)(2,1)S(1)} %bitcast.67), kind=kOutput, calls=%fused_computation.28 | convolution fusion | flops 8388608 | bytes 8585216 | tf_op jit(solution)/shard_map/ija,ijab->ijb/dot_general | solution.py:22
  69.9 2.5 collective-permute-start.2
  72.4 1.3 collective-permute-start.3
  73.7 4.2 %collective-permute-done.3 = bf16[18,1,128]{2,1,0:T(2,128)(2,1)S(1)} collective-permute-done((bf16[18,1,128]{2,1,0:T(2,128)(2,1)S(1)}, bf16[18,1,128]{2,1,0:T(2,128)(2,1)S(1)}, u32[]{:S(2)}, u32[]{:S(2)}) %collective-permute-start.3) | collective-permute-done | bytes 4640 | tf_op jit(solution)/shard_map/ppermute | solution.py:15
  78.1 0.1 rev.25
  78.4 0.2 select_select_fusion.6
  78.7 0.2 select_select_fusion.4
  78.9 0.8 multiply_reduce_fusion.6
  79.7 42.8 %psum.36 = f32[1]{0:T(128)} all-reduce(f32[1]{0:T(128)} %bitcast.14), channel_id=1, replica_groups=mesh['gx'=8,'gy'=4] {'gx','gy'}, use_global_device_ids=true, to_apply=%region_4.5 | all-reduce | flops 1 | bytes 8 | tf_op jit(solution)/shard_map/psum | solution.py:82
  122.5 1.3 multiply_reduce_fusion.5
  123.8 40.7 %psum.37 = f32[]{:T(128)} all-reduce(f32[]{:T(128)} %multiply_reduce_fusion.5), channel_id=1, replica_groups=mesh['gx'=8,'gy'=4] {'gx','gy'}, use_global_device_ids=true, to_apply=%region_6.7 | all-reduce | flops 1 | bytes 8 | tf_op jit(solution)/shard_map/psum | solution.py:85
  165.1 0.7 broadcast_divide_fusion
  165.8 1.0 fusion.16
  166.9 10.3 %all_gather.7 = f32[16,64,8]{0,2,1:T(8,128)S(1)} all-gather(f32[16,16,8]{0,2,1:T(8,128)S(1)} %fusion.16), channel_id=1, replica_groups=mesh['gx'=8,'gy'=4] {'gy'}, dimensions={1}, use_global_device_ids=true | all-gather | bytes 40960 | tf_op jit(solution)/shard_map/all_gather | solution.py:49
  177.5 0.4 fusion.37
  177.9 1.3 collective-permute-start.4
  179.2 1.3 collective-permute-start.5
  180.5 0.7 fusion.35
  181.2 2.9 collective-permute-done.5
  184.1 2.0 collective-permute-start.6
  186.2 1.3 collective-permute-start.7
  187.5 5.7 %fusion.14 = f32[16,16,1,128]{3,2,1,0:T(1,128)S(1)} fusion(bf16[16,16,128,128]{3,2,1,0:T(8,128)(2,1)} %param.17, bf16[16,16,128,1]{2,1,0,3:T(8,128)(2,1)S(1)} %bitcast.68), kind=kOutput, calls=%fused_computation.24 | convolution fusion | flops 8388608 | bytes 8585216 | tf_op jit(solution)/shard_map/ija,ijab->ijb/dot_general | solution.py:22
  193.3 0.1 select_select_fusion.3
  193.6 0.1 select_select_fusion.2
  193.8 0.1 select_select_fusion.1
  194.1 0.1 select_select_fusion
  194.2 0.9 multiply_reduce_fusion.4
  195.1 1.3 pad_maximum_fusion.22
  196.5 0.6 scatter.16
  197.1 42.6 %psum.38 = f32[2]{0:T(128)S(1)} all-reduce(f32[2]{0:T(128)S(1)} %pad_maximum_fusion.22), channel_id=1, replica_groups=mesh['gx'=8,'gy'=4] {'gx','gy'}, use_global_device_ids=true, to_apply=%region_10.11 | all-reduce | flops 2 | bytes 16 | tf_op jit(solution)/shard_map/psum | solution.py:82
  239.7 0.6 fusion.34
  240.3 2.0 multiply_reduce_fusion.2
  242.3 39.8 %psum.39 = f32[]{:T(128)} all-reduce(f32[]{:T(128)} %multiply_reduce_fusion.2), channel_id=1, replica_groups=mesh['gx'=8,'gy'=4] {'gx','gy'}, use_global_device_ids=true, to_apply=%region_12.13 | all-reduce | flops 1 | bytes 8 | tf_op jit(solution)/shard_map/psum | solution.py:85
  282.8 1.9 scatter.20
  284.7 0.8 scatter.21
  285.5 0.1 scatter.24
  285.6 0.7 fusion.33
  292.8 0.7 multiply_add_fusion
  (48 shorter events, 1.7 us)
Async XLA Ops:
  0.6 78.2 %copy-start = (bf16[4,128,128]{2,1,0:T(8,128)(2,1)S(1)}, bf16[4,128,128]{2,1,0:T(8,128)(2,1)}, u32[]{:S(2)}) copy-start(bf16[4,128,128]{2,1,0:T(8,128)(2,1)} %param.18) | copy-start | bytes 393220
  60.5 9.3 %collective-permute-start = (bf16[1,16,128]{2,1,0:T(8,128)(2,1)S(1)}, bf16[1,16,128]{2,1,0:T(8,128)(2,1)S(1)}, u32[]{:S(2)}, u32[]{:S(2)}) collective-permute-start(bf16[1,16,128]{2,1,0:T(8,128)(2,1)S(1)} %get-tuple-element.82), channel_id=1, source_target_pairs={{0,4},{4,8},{8,12},{12,16},{16,20},{20,24},{24,28},{1,5},{5,9},{9,... | collective-permute-start | bytes 12296 | tf_op jit(solution)/shard_map/ppermute | solution.py:12
  61.8 8.1 %collective-permute-start.1 = (bf16[1,16,128]{2,1,0:T(8,128)(2,1)S(1)}, bf16[1,16,128]{2,1,0:T(8,128)(2,1)S(1)}, u32[]{:S(2)}, u32[]{:S(2)}) collective-permute-start(bf16[1,16,128]{2,1,0:T(8,128)(2,1)S(1)} %get-tuple-element.83), channel_id=1, source_target_pairs={{4,0},{8,4},{12,8},{16,12},{20,16},{24,20},{28,24},{5,1},{9,5},{13... | collective-permute-start | bytes 12296 | tf_op jit(solution)/shard_map/ppermute | solution.py:15
  64.1 58.4 %copy-start.1 = (f32[16,16,128]{2,1,0:T(8,128)S(1)}, f32[16,16,128]{2,1,0:T(8,128)}, u32[]{:S(2)}) copy-start(f32[16,16,128]{2,1,0:T(8,128)} %param.16) | copy-start | bytes 393220
  64.1 101.7 %copy-start.3 = (f32[128,8]{0,1:T(8,128)S(1)}, f32[128,8]{0,1:T(8,128)}, u32[]{:S(2)}) copy-start(f32[128,8]{0,1:T(8,128)} %param.20) | copy-start | bytes 12292
  64.1 113.3 %copy-start.2 = (f32[16,16,8,8]{1,3,2,0:T(8,128)S(1)}, f32[16,16,8,8]{1,3,2,0:T(8,128)}, u32[]{:S(2)}) copy-start(f32[16,16,8,8]{1,3,2,0:T(8,128)} %param.21) | copy-start | bytes 196612
  69.9 3.8 %collective-permute-start.2 = (bf16[18,1,128]{2,1,0:T(2,128)(2,1)S(1)}, bf16[18,1,128]{2,1,0:T(2,128)(2,1)S(1)}, u32[]{:S(2)}, u32[]{:S(2)}) collective-permute-start(bf16[18,1,128]{2,1,0:T(2,128)(2,1)S(1)} %get-tuple-element.74), channel_id=1, source_target_pairs={{0,1},{1,2},{2,3},{4,5},{5,6},{6,7},{8,9},{9,10},{10,11},{12,13},{... | collective-permute-start | bytes 13832 | tf_op jit(solution)/shard_map/ppermute | solution.py:12
  72.4 5.6 %collective-permute-start.3 = (bf16[18,1,128]{2,1,0:T(2,128)(2,1)S(1)}, bf16[18,1,128]{2,1,0:T(2,128)(2,1)S(1)}, u32[]{:S(2)}, u32[]{:S(2)}) collective-permute-start(bf16[18,1,128]{2,1,0:T(2,128)(2,1)S(1)} %get-tuple-element.75), channel_id=1, source_target_pairs={{1,0},{2,1},{3,2},{5,4},{6,5},{7,6},{9,8},{10,9},{11,10},{13,12},{... | collective-permute-start | bytes 13832 | tf_op jit(solution)/shard_map/ppermute | solution.py:15
  177.9 3.3 %collective-permute-start.4 = (bf16[1,16,128]{2,1,0:T(8,128)(2,1)S(1)}, bf16[1,16,128]{2,1,0:T(8,128)(2,1)S(1)}, u32[]{:S(2)}, u32[]{:S(2)}) collective-permute-start(bf16[1,16,128]{2,1,0:T(8,128)(2,1)S(1)} %get-tuple-element.80), channel_id=1, source_target_pairs={{0,4},{4,8},{8,12},{12,16},{16,20},{20,24},{24,28},{1,5},{5,9},{9,... | collective-permute-start | bytes 12296 | tf_op jit(solution)/shard_map/ppermute | solution.py:12
  179.2 4.9 %collective-permute-start.5 = (bf16[1,16,128]{2,1,0:T(8,128)(2,1)S(1)}, bf16[1,16,128]{2,1,0:T(8,128)(2,1)S(1)}, u32[]{:S(2)}, u32[]{:S(2)}) collective-permute-start(bf16[1,16,128]{2,1,0:T(8,128)(2,1)S(1)} %get-tuple-element.81), channel_id=1, source_target_pairs={{4,0},{8,4},{12,8},{16,12},{20,16},{24,20},{28,24},{5,1},{9,5},{13... | collective-permute-start | bytes 12296 | tf_op jit(solution)/shard_map/ppermute | solution.py:15
  184.1 9.0 %collective-permute-start.6 = (bf16[18,1,128]{2,1,0:T(2,128)(2,1)S(1)}, bf16[18,1,128]{2,1,0:T(2,128)(2,1)S(1)}, u32[]{:S(2)}, u32[]{:S(2)}) collective-permute-start(bf16[18,1,128]{2,1,0:T(2,128)(2,1)S(1)} %get-tuple-element.70), channel_id=1, source_target_pairs={{0,1},{1,2},{2,3},{4,5},{5,6},{6,7},{8,9},{9,10},{10,11},{12,13},{... | collective-permute-start | bytes 13832 | tf_op jit(solution)/shard_map/ppermute | solution.py:12
  186.2 7.0 %collective-permute-start.7 = (bf16[18,1,128]{2,1,0:T(2,128)(2,1)S(1)}, bf16[18,1,128]{2,1,0:T(2,128)(2,1)S(1)}, u32[]{:S(2)}, u32[]{:S(2)}) collective-permute-start(bf16[18,1,128]{2,1,0:T(2,128)(2,1)S(1)} %get-tuple-element.71), channel_id=1, source_target_pairs={{1,0},{2,1},{3,2},{5,4},{6,5},{7,6},{9,8},{10,9},{11,10},{13,12},{... | collective-permute-start | bytes 13832 | tf_op jit(solution)/shard_map/ppermute | solution.py:15
  285.6 7.9 %copy-start.4 = (f32[3,2]{0,1:T(2,128)}, f32[3,2]{0,1:T(2,128)S(1)}, u32[]{:S(2)}) copy-start(f32[3,2]{0,1:T(2,128)S(1)} %scatter.24) | copy-start | bytes 76
where the time goes:
time: 295 us; the launch traced here: 293 us
  blocking collectives  228 us (77%)
  matrix products  17.3 us (6%)
  starting transfers between devices  12.2 us (4%)
  other arithmetic  11 us (4%)
  between operations  9.67 us (3%)
  local copies, waits for them, and re-layouts  7.55 us (3%)
  waiting for transfers between devices  7.18 us (2%)
    psum x2, blocking collectives, body(): coeffs = lax.psum(partial_dots, ('gx', 'gy'))  85.4 us
    psum x2, blocking collectives, body(): length = jnp.sqrt(lax.psum(jnp.sum(image * image), ('gx', 'gy')))  80.4 us
    psum x1, blocking collectives, body(): start_len = jnp.sqrt(lax.psum(jnp.sum(rhs_field * rhs_field), ('gx', 'gy')))  42.2 us
    all_gather x2, blocking collectives, coarse_correct(): column = lax.all_gather(coarse, 'gy', axis=1, tiled=True)  20.6 us
    dot_general x2, matrix products, apply_operator(): jnp.einsum('ija,ijab->ijb', rounded, diag_blocks, preferred_element_type=...  11.4 us
    ppermute x4, waiting for transfers between devices, padded_2(): lax.ppermute(lax.slice_in_dim(block, 0, width, axis=dim), axis, backward)  7.11 us
    ppermute x4, starting transfers between devices, padded_2(): lax.ppermute(lax.slice_in_dim(block, block.shape[dim] - width, None, axis...  7.05 us
  transfers between devices with their start and end apart: 8, of which 2 were waited for; matrix products, arithmetic and copies ran while one was open for 4% of the time, Pallas kernels for 0%

commit v1 on v0

--- a/solution.py
+++ b/solution.py
@@ -79,7 +79,8 @@
         precon.append(precond)
         image = apply_operator(precond, diag_blocks, face_lift, face_state)
         partial_dots = jnp.stack([jnp.sum(vector * image) for vector in basis])
-        coeffs = lax.psum(partial_dots, ("gx", "gy"))
+        read_figure = lambda arr_in: lax.psum(lax.psum(arr_in, axis_name="gy"), axis_name="gx")
+        coeffs = read_figure(partial_dots)
         for index in range(step + 1):
             image = image - coeffs[index] * basis[index]
         length = jnp.sqrt(lax.psum(jnp.sum(image * image), ("gx", "gy")))

time: 295 us -> 258 us (0.87)
  blocking collectives: 228 us -> 188 us
    psum x2 -> x4, blocking collectives: 85.4 us -> 49.7 us  [the longest x2 29.1 us: body(): lax.psum(lax.psum(arr_in, axis_name='gy'), axis_name='gx')]
    psum x2, blocking collectives: 80.4 us -> 75.7 us  [body(): length = jnp.sqrt(lax.psum(jnp.sum(image * image), ('gx', 'gy')))]
  transfers between devices with their start and end apart: 8 -> 8, of which waited for: 2 -> 2; matrix products, arithmetic and copies ran while one was open for 4% -> 5% of each run, Pallas kernels for 0% -> 0%
where the time goes in v1:
time: 258 us; the launch traced here: 256 us
  blocking collectives  188 us (73%)
  matrix products  17.4 us (7%)
  starting transfers between devices  13.6 us (5%)
  other arithmetic  11.1 us (4%)
  between operations  9.67 us (4%)
  waiting for transfers between devices  8.36 us (3%)
  local copies, waits for them, and re-layouts  7.47 us (3%)
    psum x2, blocking collectives, body(): length = jnp.sqrt(lax.psum(jnp.sum(image * image), ('gx', 'gy')))  75.7 us
    psum x1, blocking collectives, body(): start_len = jnp.sqrt(lax.psum(jnp.sum(rhs_field * rhs_field), ('gx', 'gy')))  42.2 us
    psum x2, blocking collectives, body(): lax.psum(lax.psum(arr_in, axis_name='gy'), axis_name='gx')  29.1 us
    all_gather x2, blocking collectives, coarse_correct(): column = lax.all_gather(coarse, 'gy', axis=1, tiled=True)  20.6 us
    psum x2, blocking collectives, body(): lax.psum(arr_in, axis_name='gy')  20.5 us
    dot_general x2, matrix products, apply_operator(): jnp.einsum('ija,ijab->ijb', rounded, diag_blocks, preferred_element_type=...  11.4 us
    ppermute x4, starting transfers between devices, padded_2(): lax.ppermute(lax.slice_in_dim(block, block.shape[dim] - width, None, axis...  8.41 us
    ppermute x4, waiting for transfers between devices, padded_2(): lax.ppermute(lax.slice_in_dim(block, 0, width, axis=dim), axis, backward)  8.3 us
  transfers between devices with their start and end apart: 8, of which 2 were waited for; matrix products, arithmetic and copies ran while one was open for 5% of the time, Pallas kernels for 0%

profile of v1, /device:TPU:0, one launch (start us, length us, event | category | flops | bytes accessed | tf_op | source)
XLA Modules:
  0.0 255.6 jit_solution(16129806525222211507)
XLA Ops:
  0.6 1.6 multiply_reduce_fusion.7
  2.2 42.2 %psum.49 = f32[]{:T(128)} all-reduce(f32[]{:T(128)} %multiply_reduce_fusion.7), channel_id=1, replica_groups=mesh['gx'=8,'gy'=4] {'gx','gy'}, use_global_device_ids=true, to_apply=%region_1.0 | all-reduce | flops 1 | bytes 8 | tf_op jit(solution)/shard_map/psum | solution.py:73
  45.1 0.9 broadcast_divide_fusion.1
  46.0 1.7 fusion.20
  47.7 10.3 %all_gather.6 = f32[16,64,8]{0,2,1:T(8,128)S(1)} all-gather(f32[16,16,8]{0,2,1:T(8,128)S(1)} %fusion.20), channel_id=1, replica_groups=mesh['gx'=8,'gy'=4] {'gy'}, dimensions={1}, use_global_device_ids=true | all-gather | bytes 40960 | tf_op jit(solution)/shard_map/all_gather | solution.py:49
  58.3 1.1 multiply_reduce_fusion.1
  59.4 1.1 fusion.36
  60.5 1.3 collective-permute-start
  61.8 1.3 collective-permute-start.1
  63.1 0.9 fusion.32
  64.1 5.7 %fusion.18 = f32[16,16,1,128]{3,2,1,0:T(1,128)S(1)} fusion(bf16[16,16,128,128]{3,2,1,0:T(8,128)(2,1)} %param.17, bf16[16,16,128,1]{2,1,0,3:T(8,128)(2,1)S(1)} %bitcast.67), kind=kOutput, calls=%fused_computation.28 | convolution fusion | flops 8388608 | bytes 8585216 | tf_op jit(solution)/shard_map/ija,ijab->ijb/dot_general | solution.py:22
  69.9 2.5 collective-permute-start.2
  72.4 1.3 collective-permute-start.3
  73.7 4.2 %collective-permute-done.3 = bf16[18,1,128]{2,1,0:T(2,128)(2,1)S(1)} collective-permute-done((bf16[18,1,128]{2,1,0:T(2,128)(2,1)S(1)}, bf16[18,1,128]{2,1,0:T(2,128)(2,1)S(1)}, u32[]{:S(2)}, u32[]{:S(2)}) %collective-permute-start.3) | collective-permute-done | bytes 4640 | tf_op jit(solution)/shard_map/ppermute | solution.py:15
  78.4 0.2 select_select_fusion.6
  78.7 0.2 select_select_fusion.4
  78.9 0.8 multiply_reduce_fusion.6
  79.7 10.4 %psum.50 = f32[1]{0:T(128)} all-reduce(f32[1]{0:T(128)} %bitcast.14), channel_id=1, replica_groups=mesh['gx'=8,'gy'=4] {'gy'}, use_global_device_ids=true, to_apply=%region_4.5 | all-reduce | flops 1 | bytes 8 | tf_op jit(solution)/shard_map/psum | solution.py:82
  90.1 15.5 %psum.51 = f32[1]{0:T(128)} all-reduce(f32[1]{0:T(128)} %psum.50), channel_id=1, replica_groups=mesh['gx'=8,'gy'=4] {'gx'}, use_global_device_ids=true, to_apply=%region_5.6 | all-reduce | flops 1 | bytes 8 | tf_op jit(solution)/shard_map/psum | solution.py:82
  105.6 1.3 multiply_reduce_fusion.5
  106.9 37.8 %psum.52 = f32[]{:T(128)} all-reduce(f32[]{:T(128)} %multiply_reduce_fusion.5), channel_id=1, replica_groups=mesh['gx'=8,'gy'=4] {'gx','gy'}, use_global_device_ids=true, to_apply=%region_7.8 | all-reduce | flops 1 | bytes 8 | tf_op jit(solution)/shard_map/psum | solution.py:86
  145.4 0.7 broadcast_divide_fusion
  146.1 1.0 fusion.16
  147.1 10.3 %all_gather.7 = f32[16,64,8]{0,2,1:T(8,128)S(1)} all-gather(f32[16,16,8]{0,2,1:T(8,128)S(1)} %fusion.16), channel_id=1, replica_groups=mesh['gx'=8,'gy'=4] {'gy'}, dimensions={1}, use_global_device_ids=true | all-gather | bytes 40960 | tf_op jit(solution)/shard_map/all_gather | solution.py:49
  157.7 0.4 fusion.37
  158.2 1.3 collective-permute-start.4
  159.5 1.3 collective-permute-start.5
  160.8 4.1 %collective-permute-done.5 = bf16[1,16,128]{2,1,0:T(8,128)(2,1)S(1)} collective-permute-done((bf16[1,16,128]{2,1,0:T(8,128)(2,1)S(1)}, bf16[1,16,128]{2,1,0:T(8,128)(2,1)S(1)}, u32[]{:S(2)}, u32[]{:S(2)}) %collective-permute-start.5) | collective-permute-done | bytes 4128 | tf_op jit(solution)/shard_map/ppermute | solution.py:15
  164.9 3.4 %collective-permute-start.6 = (bf16[18,1,128]{2,1,0:T(2,128)(2,1)S(1)}, bf16[18,1,128]{2,1,0:T(2,128)(2,1)S(1)}, u32[]{:S(2)}, u32[]{:S(2)}) collective-permute-start(bf16[18,1,128]{2,1,0:T(2,128)(2,1)S(1)} %get-tuple-element.70), channel_id=1, source_target_pairs={{0,1},{1,2},{2,3},{4,5},{5,6},{6,7},{8,9},{9,10},{10,11},{12,13},{... | collective-permute-start | bytes 13832 | tf_op jit(solution)/shard_map/ppermute | solution.py:12
  168.3 1.3 collective-permute-start.7
  169.6 5.7 %fusion.14 = f32[16,16,1,128]{3,2,1,0:T(1,128)S(1)} fusion(bf16[16,16,128,128]{3,2,1,0:T(8,128)(2,1)} %param.17, bf16[16,16,128,1]{2,1,0,3:T(8,128)(2,1)S(1)} %bitcast.68), kind=kOutput, calls=%fused_computation.24 | convolution fusion | flops 8388608 | bytes 8585216 | tf_op jit(solution)/shard_map/ija,ijab->ijb/dot_general | solution.py:22
  175.4 0.1 select_select_fusion.3
  175.7 0.1 select_select_fusion.2
  175.9 0.1 select_select_fusion.1
  176.2 0.1 select_select_fusion
  176.3 0.9 multiply_reduce_fusion.4
  177.2 1.3 pad_maximum_fusion.22
  178.6 0.6 fusion.35
  179.1 10.1 %psum.53 = f32[2]{0:T(128)S(1)} all-reduce(f32[2]{0:T(128)S(1)} %pad_maximum_fusion.22), channel_id=1, replica_groups=mesh['gx'=8,'gy'=4] {'gy'}, use_global_device_ids=true, to_apply=%region_11.12 | all-reduce | flops 2 | bytes 16 | tf_op jit(solution)/shard_map/psum | solution.py:82
  189.2 0.6 scatter.16
  189.9 13.7 %psum.54 = f32[2]{0:T(128)S(1)} all-reduce(f32[2]{0:T(128)S(1)} %psum.53), channel_id=1, replica_groups=mesh['gx'=8,'gy'=4] {'gx'}, use_global_device_ids=true, to_apply=%region_12.13 | all-reduce | flops 2 | bytes 16 | tf_op jit(solution)/shard_map/psum | solution.py:82
  203.5 0.6 fusion.34
  204.1 2.0 multiply_reduce_fusion.2
  206.3 38.0 %psum.55 = f32[]{:T(128)} all-reduce(f32[]{:T(128)} %multiply_reduce_fusion.2), channel_id=1, replica_groups=mesh['gx'=8,'gy'=4] {'gx','gy'}, use_global_device_ids=true, to_apply=%region_14.15 | all-reduce | flops 1 | bytes 8 | tf_op jit(solution)/shard_map/psum | solution.py:86
  244.9 1.9 scatter.20
  246.9 0.8 scatter.21
  247.8 0.7 fusion.33
  255.0 0.7 multiply_add_fusion
  (50 shorter events, 1.9 us)
Async XLA Ops:
  0.6 78.2 %copy-start = (bf16[4,128,128]{2,1,0:T(8,128)(2,1)S(1)}, bf16[4,128,128]{2,1,0:T(8,128)(2,1)}, u32[]{:S(2)}) copy-start(bf16[4,128,128]{2,1,0:T(8,128)(2,1)} %param.18) | copy-start | bytes 393220
  60.5 9.3 %collective-permute-start = (bf16[1,16,128]{2,1,0:T(8,128)(2,1)S(1)}, bf16[1,16,128]{2,1,0:T(8,128)(2,1)S(1)}, u32[]{:S(2)}, u32[]{:S(2)}) collective-permute-start(bf16[1,16,128]{2,1,0:T(8,128)(2,1)S(1)} %get-tuple-element.82), channel_id=1, source_target_pairs={{0,4},{4,8},{8,12},{12,16},{16,20},{20,24},{24,28},{1,5},{5,9},{9,... | collective-permute-start | bytes 12296 | tf_op jit(solution)/shard_map/ppermute | solution.py:12
  61.8 8.1 %collective-permute-start.1 = (bf16[1,16,128]{2,1,0:T(8,128)(2,1)S(1)}, bf16[1,16,128]{2,1,0:T(8,128)(2,1)S(1)}, u32[]{:S(2)}, u32[]{:S(2)}) collective-permute-start(bf16[1,16,128]{2,1,0:T(8,128)(2,1)S(1)} %get-tuple-element.83), channel_id=1, source_target_pairs={{4,0},{8,4},{12,8},{16,12},{20,16},{24,20},{28,24},{5,1},{9,5},{13... | collective-permute-start | bytes 12296 | tf_op jit(solution)/shard_map/ppermute | solution.py:15
  64.1 41.5 %copy-start.1 = (f32[16,16,128]{2,1,0:T(8,128)S(1)}, f32[16,16,128]{2,1,0:T(8,128)}, u32[]{:S(2)}) copy-start(f32[16,16,128]{2,1,0:T(8,128)} %param.16) | copy-start | bytes 393220
  64.1 81.9 %copy-start.3 = (f32[128,8]{0,1:T(8,128)S(1)}, f32[128,8]{0,1:T(8,128)}, u32[]{:S(2)}) copy-start(f32[128,8]{0,1:T(8,128)} %param.20) | copy-start | bytes 12292
  64.1 93.5 %copy-start.2 = (f32[16,16,8,8]{1,3,2,0:T(8,128)S(1)}, f32[16,16,8,8]{1,3,2,0:T(8,128)}, u32[]{:S(2)}) copy-start(f32[16,16,8,8]{1,3,2,0:T(8,128)} %param.21) | copy-start | bytes 196612
  69.9 3.8 %collective-permute-start.2 = (bf16[18,1,128]{2,1,0:T(2,128)(2,1)S(1)}, bf16[18,1,128]{2,1,0:T(2,128)(2,1)S(1)}, u32[]{:S(2)}, u32[]{:S(2)}) collective-permute-start(bf16[18,1,128]{2,1,0:T(2,128)(2,1)S(1)} %get-tuple-element.74), channel_id=1, source_target_pairs={{0,1},{1,2},{2,3},{4,5},{5,6},{6,7},{8,9},{9,10},{10,11},{12,13},{... | collective-permute-start | bytes 13832 | tf_op jit(solution)/shard_map/ppermute | solution.py:12
  72.4 5.6 %collective-permute-start.3 = (bf16[18,1,128]{2,1,0:T(2,128)(2,1)S(1)}, bf16[18,1,128]{2,1,0:T(2,128)(2,1)S(1)}, u32[]{:S(2)}, u32[]{:S(2)}) collective-permute-start(bf16[18,1,128]{2,1,0:T(2,128)(2,1)S(1)} %get-tuple-element.75), channel_id=1, source_target_pairs={{1,0},{2,1},{3,2},{5,4},{6,5},{7,6},{9,8},{10,9},{11,10},{13,12},{... | collective-permute-start | bytes 13832 | tf_op jit(solution)/shard_map/ppermute | solution.py:15
  158.2 2.6 %collective-permute-start.4 = (bf16[1,16,128]{2,1,0:T(8,128)(2,1)S(1)}, bf16[1,16,128]{2,1,0:T(8,128)(2,1)S(1)}, u32[]{:S(2)}, u32[]{:S(2)}) collective-permute-start(bf16[1,16,128]{2,1,0:T(8,128)(2,1)S(1)} %get-tuple-element.80), channel_id=1, source_target_pairs={{0,4},{4,8},{8,12},{12,16},{16,20},{20,24},{24,28},{1,5},{5,9},{9,... | collective-permute-start | bytes 12296 | tf_op jit(solution)/shard_map/ppermute | solution.py:12
  159.5 5.4 %collective-permute-start.5 = (bf16[1,16,128]{2,1,0:T(8,128)(2,1)S(1)}, bf16[1,16,128]{2,1,0:T(8,128)(2,1)S(1)}, u32[]{:S(2)}, u32[]{:S(2)}) collective-permute-start(bf16[1,16,128]{2,1,0:T(8,128)(2,1)S(1)} %get-tuple-element.81), channel_id=1, source_target_pairs={{4,0},{8,4},{12,8},{16,12},{20,16},{24,20},{28,24},{5,1},{9,5},{13... | collective-permute-start | bytes 12296 | tf_op jit(solution)/shard_map/ppermute | solution.py:15
  164.9 10.3 %collective-permute-start.6 = (bf16[18,1,128]{2,1,0:T(2,128)(2,1)S(1)}, bf16[18,1,128]{2,1,0:T(2,128)(2,1)S(1)}, u32[]{:S(2)}, u32[]{:S(2)}) collective-permute-start(bf16[18,1,128]{2,1,0:T(2,128)(2,1)S(1)} %get-tuple-element.70), channel_id=1, source_target_pairs={{0,1},{1,2},{2,3},{4,5},{5,6},{6,7},{8,9},{9,10},{10,11},{12,13},{... | collective-permute-start | bytes 13832 | tf_op jit(solution)/shard_map/ppermute | solution.py:12
  168.3 7.0 %collective-permute-start.7 = (bf16[18,1,128]{2,1,0:T(2,128)(2,1)S(1)}, bf16[18,1,128]{2,1,0:T(2,128)(2,1)S(1)}, u32[]{:S(2)}, u32[]{:S(2)}) collective-permute-start(bf16[18,1,128]{2,1,0:T(2,128)(2,1)S(1)} %get-tuple-element.71), channel_id=1, source_target_pairs={{1,0},{2,1},{3,2},{5,4},{6,5},{7,6},{9,8},{10,9},{11,10},{13,12},{... | collective-permute-start | bytes 13832 | tf_op jit(solution)/shard_map/ppermute | solution.py:15
  247.8 7.9 %copy-start.4 = (f32[3,2]{0,1:T(2,128)}, f32[3,2]{0,1:T(2,128)S(1)}, u32[]{:S(2)}) copy-start(f32[3,2]{0,1:T(2,128)S(1)} %scatter.24) | copy-start | bytes 76
